TPU v7x, 32 devices: a whole 2x2x4 slice. The times are simulated.
32 devices in a mesh: row: 4 (over z), col: 4 (over y, core), depth: 2 (over x).
Axes of the slice: x: 2, y: 2, z: 4, core: 2. Of those that a mesh axis runs over, the one named last changes fastest.
Arguments:
- tokens: bfloat16 [256, 12288], P(('row', 'col'), 'depth'), may hold values from -6 to 6
- in_weight: bfloat16 [12288, 49152], P('depth', ('row', 'col')), may hold values from -0.0546875 to 0.0546875
- in_bias: bfloat16 [49152], P(('row', 'col')), may hold values from -4 to 4
- out_weight: bfloat16 [49152, 12288], P(('row', 'col'), 'depth'), may hold values from -0.02734375 to 0.02734375
- out_bias: bfloat16 [12288], P('depth'), may hold values from -3 to 3
Outputs:
- outputs: bfloat16 [256, 12288], P(('row', 'col'), 'depth')
All inputs are finite; a program needn't handle non-finite values.
Results may differ from a plain program's by a relative error of at most 0.0045.
Values may be sent and summed in bfloat16 or wider, within the bound.
A program may use at most 192 MiB of HBM per device.

v0:
```python
import jax
import jax.numpy as jnp
from jax import lax
from jax.sharding import PartitionSpec as P


def body(tokens, in_weight, in_bias, out_weight, out_bias):
    partial_value = jnp.dot(
        lax.all_gather(tokens, ("row", "col"), axis=0, tiled=True),
        in_weight,
        preferred_element_type=jnp.float32,
    )
    bias_row = in_bias.astype(jnp.float32)
    summed = lax.psum(partial_value, "depth")
    hidden = jax.nn.gelu(summed + bias_row, approximate=True).astype(jnp.bfloat16)
    outputs = lax.psum_scatter(
        jnp.dot(hidden, out_weight, preferred_element_type=jnp.float32),
        ("row", "col"),
        scatter_dimension=0,
        tiled=True,
    )
    return (outputs + out_bias.astype(jnp.float32)).astype(jnp.bfloat16)


def solution(mesh):
    in_specs = (
        P(("row", "col"), "depth"),
        P("depth", ("row", "col")),
        P(("row", "col")),
        P(("row", "col"), "depth"),
        P("depth"),
    )
    out_specs = P(("row", "col"), "depth")
    return jax.shard_map(body, mesh=mesh, in_specs=in_specs, out_specs=out_specs, check_vma=False)
```

profile of v0, /device:TPU:0, one launch (start us, length us, event | category | flops | bytes accessed | tf_op | source)
XLA Modules:
  0.0 274.8 jit_solution(7004497836152599166)
XLA Ops:
  6.5 0.0 all-gather.2.cloned.1.call-start
  6.5 0.7 all-gather.2.cloned.1.call-update
  7.3 0.0 all-reduce.2.cloned.1.call-start
  7.3 50.3 %all-gather.2.cloned.1.call-done = bf16[256,6144]{1,0:T(8,128)(2,1)} async-done(((bf16[16,6144]{1,0:T(8,128)(2,1)}), bf16[256,6144]{1,0:T(8,128)(2,1)}) %all-gather.2.cloned.1.call-update) | async-done | bytes 3145744 | tf_op jit(solution)/shard_map/all_gather | solution.py:9
  57.6 18.8 %fusion.19 = f32[256,3072]{1,0:T(8,128)} fusion(bf16[256,6144]{1,0:T(8,128)(2,1)} %all-gather.2.cloned.1.call-done, bf16[6144,3072]{1,0:T(8,128)(2,1)} %param.6), kind=kOutput, calls=%fused_computation.20 | convolution fusion | flops 9663676416 | bytes 44040192 | tf_op jit(solution)/shard_map/dot_general | solution.py:8
  76.4 0.0 copy-start.1
  76.4 0.0 all-reduce.2.cloned.1.call-update
  76.4 0.0 reduce-scatter.2.cloned.1.call-start
  76.5 0.6 copy-done.1
  77.1 84.1 %all-reduce.2.cloned.1.call-done = f32[256,3072]{1,0:T(8,128)} async-done(((f32[256,3072]{1,0:T(8,128)}), f32[256,3072]{1,0:T(8,128)}) %all-reduce.2.cloned.1.call-update) | async-done | bytes 3145744 | tf_op jit(solution)/shard_map/psum | solution.py:14
  161.1 19.9 %fusion.8 = f32[256,6144]{1,0:T(8,128)} fusion(bf16[3072,6144]{1,0:T(8,128)(2,1)} %param.8, f32[256,3072]{1,0:T(8,128)} %all-reduce.2.cloned.1.call-done, f32[3072]{0:T(1024)S(1)} %convert_element_type.12), kind=kOutput, calls=%fused_computation.9 | convolution fusion | flops 9671540736 | bytes 47198208 | tf_op jit(solution)/shard_map/dot_general | solution.py:17
  181.1 0.0 copy-start
  181.1 0.0 reduce-scatter.2.cloned.1.call-update
  181.1 0.7 copy-done
  181.8 84.7 %reduce-scatter.2.cloned.1.call-done = f32[16,6144]{1,0:T(8,128)} async-done(((f32[256,6144]{1,0:T(8,128)}), f32[16,6144]{1,0:T(8,128)}) %reduce-scatter.2.cloned.1.call-update) | async-done | bytes 393232 | tf_op jit(solution)/shard_map/reduce_scatter | solution.py:16
  266.5 1.7 add_convert_fusion
  (2 shorter events, 0.0 us)
Async XLA Ops:
  6.5 51.0 %all-gather.2.cloned.1.call-start = ((), (), s32[]{:S(2)}) async-start(), calls=%async_computation.1 | async-start | bytes 3342336 | tf_op jit(solution)/shard_map/all_gather | solution.py:9
  7.3 153.9 %all-reduce.2.cloned.1.call-start = ((), (), s32[]{:S(2)}) async-start(), calls=%async_computation.2 | async-start | bytes 6291456 | tf_op jit(solution)/shard_map/psum | solution.py:14
  76.4 0.7 copy-start.1
  76.4 190.1 %reduce-scatter.2.cloned.1.call-start = ((), (), s32[]{:S(2)}) async-start(), calls=%async_computation.3 | async-start | bytes 6684672 | tf_op jit(solution)/shard_map/reduce_scatter | solution.py:16
  181.1 0.7 copy-start
Sparse Core Ops, SparseCore 0:
  9.6 47.8 all-gather.1
  76.5 84.5 all-reduce.1
  181.2 85.2 reduce-scatter.1
where the time goes:
time: 275 us
  waiting for transfers between devices  220 us (80%)
  matrix products  38.8 us (14%)
  between operations  13.1 us (5%)
    reduce_scatter x1, waiting for transfers between devices, body(): lax.psum_scatter(jnp.dot(hidden, out_weight, preferred_element_type=jnp.f...  84.7 us
    psum x1, waiting for transfers between devices, body(): summed = lax.psum(partial_value, 'depth')  84.1 us
    all_gather x1, waiting for transfers between devices, body(): lax.all_gather(tokens, ('row', 'col'), axis=0, tiled=True)  50.3 us
    dot_general x1, matrix products, body(): jnp.dot(hidden, out_weight, preferred_element_type=jnp.float32)  19.9 us
    dot_general x1, matrix products, body(): jnp.dot(lax.all_gather(tokens, ('row', 'col'), axis=0, tiled=True), in_we...  18.8 us
  transfers between devices with their start and end apart: 3, of which 3 were waited for; matrix products, arithmetic and copies ran while one was open for 0% of the time, Pallas kernels for 0%

commit v1 on v0

--- a/solution.py
+++ b/solution.py
@@ -4,11 +4,21 @@
 from jax.sharding import PartitionSpec as P
 
 
+def doubled_up(x, axis, dim):
+    ways, here, step = (lax.axis_size(axis), lax.axis_index(axis), x.shape[dim])
+    line, have = (x, 1)
+    while have < ways:
+        line = jnp.concatenate(
+            [line, lax.ppermute(line, axis, [(d, (d - have) % ways) for d in range(ways)])],
+            axis=dim,
+        )
+        have = 2 * have
+    return jnp.roll(line, here * step, axis=dim)
+
+
 def body(tokens, in_weight, in_bias, out_weight, out_bias):
     partial_value = jnp.dot(
-        lax.all_gather(tokens, ("row", "col"), axis=0, tiled=True),
-        in_weight,
-        preferred_element_type=jnp.float32,
+        doubled_up(tokens, ("row", "col"), 0), in_weight, preferred_element_type=jnp.float32
     )
     bias_row = in_bias.astype(jnp.float32)
     summed = lax.psum(partial_value, "depth")

time: 275 us -> 342 us (1.24)
  waiting for transfers between devices: 220 us -> 266 us
  local copies, waits for them, and re-layouts: 1.3 us -> 11 us
  starting transfers between devices: 0.08 us -> 8.02 us
    ppermute x0 -> x4, waiting for transfers between devices: none -> 97.5 us  [doubled_up(): lax.ppermute(line, axis, [(d, (d - have) % ways) for d in range(ways)])]
    all_gather x1 -> x0, waiting for transfers between devices: 50.3 us -> none  [body(): lax.all_gather(tokens, ('row', 'col'), axis=0, tiled=True)]
    unnamed x4 -> x15, local copies, waits for them, and re-layouts: 1.3 us -> 9.67 us
    ppermute x0 -> x4, starting transfers between devices: none -> 7.97 us  [doubled_up(): lax.ppermute(line, axis, [(d, (d - have) % ways) for d in range(ways)])]
  transfers between devices with their start and end apart: 3 -> 6, of which waited for: 3 -> 6; matrix products, arithmetic and copies ran while one was open for 0% -> 1% of each run, Pallas kernels for 0% -> 0%
where the time goes in v1:
time: 342 us
  waiting for transfers between devices  266 us (78%)
  matrix products  38.8 us (11%)
  between operations  13.4 us (4%)
  local copies, waits for them, and re-layouts  11 us (3%)
  starting transfers between devices  8.02 us (2%)
  other arithmetic  4.68 us (1%)
    ppermute x4, waiting for transfers between devices, doubled_up(): lax.ppermute(line, axis, [(d, (d - have) % ways) for d in range(ways)])  97.5 us
    reduce_scatter x1, waiting for transfers between devices, body(): lax.psum_scatter(jnp.dot(hidden, out_weight, preferred_element_type=jnp.f...  84.7 us
    psum x1, waiting for transfers between devices, body(): summed = lax.psum(partial_value, 'depth')  83.5 us
    dot_general x1, matrix products, body(): jnp.dot(hidden, out_weight, preferred_element_type=jnp.float32)  20 us
    dot_general x1, matrix products, body(): jnp.dot(doubled_up(tokens, ('row', 'col'), 0), in_weight, preferred_eleme...  18.8 us
    unnamed x15, local copies, waits for them, and re-layouts  9.67 us
    ppermute x4, starting transfers between devices, doubled_up(): lax.ppermute(line, axis, [(d, (d - have) % ways) for d in range(ways)])  7.97 us
  transfers between devices with their start and end apart: 6, of which 6 were waited for; matrix products, arithmetic and copies ran while one was open for 1% of the time, Pallas kernels for 0%

profile of v1, /device:TPU:0, one launch (start us, length us, event | category | flops | bytes accessed | tf_op | source)
XLA Modules:
  0.0 341.6 jit_solution(5993452394209728028)
XLA Ops:
  6.5 0.0 all-reduce.2.cloned.1.call-start
  6.5 5.4 %collective-permute-start = (bf16[16,6144]{1,0:T(8,128)(2,1)}, bf16[16,6144]{1,0:T(8,128)(2,1)S(1)}, u32[]{:S(2)}, u32[]{:S(2)}) collective-permute-start(bf16[16,6144]{1,0:T(8,128)(2,1)} %param.5), channel_id=1, source_target_pairs={{0,30},{2,0},{4,2},{6,4},{8,6},{10,8},{12,10},{14,12},{16,14},{18,... | collective-permute-start | bytes 589832 | tf_op jit(solution)/shard_map/ppermute | solution.py:12
  12.0 3.5 %collective-permute-done = bf16[16,6144]{1,0:T(8,128)(2,1)S(1)} collective-permute-done((bf16[16,6144]{1,0:T(8,128)(2,1)}, bf16[16,6144]{1,0:T(8,128)(2,1)S(1)}, u32[]{:S(2)}, u32[]{:S(2)}) %collective-permute-start) | collective-permute-done | bytes 196640 | tf_op jit(solution)/shard_map/ppermute | solution.py:12
  15.5 1.0 pad_maximum_fusion.2
  16.4 0.6 collective-permute-start.1
  17.1 8.8 %collective-permute-done.1 = bf16[32,6144]{1,0:T(8,128)(2,1)S(1)} collective-permute-done((bf16[32,6144]{1,0:T(8,128)(2,1)S(1)}, bf16[32,6144]{1,0:T(8,128)(2,1)S(1)}, u32[]{:S(2)}, u32[]{:S(2)}) %collective-permute-start.1) | collective-permute-done | bytes 393248 | tf_op jit(solution)/shard_map/ppermute | solution.py:12
  25.8 1.0 pad_maximum_fusion.1
  26.8 0.8 collective-permute-start.2
  27.6 1.6 constant_dynamic-update-slice_fusion.9
  29.2 17.9 %collective-permute-done.2 = bf16[64,6144]{1,0:T(8,128)(2,1)S(1)} collective-permute-done((bf16[64,6144]{1,0:T(8,128)(2,1)S(1)}, bf16[64,6144]{1,0:T(8,128)(2,1)S(1)}, u32[]{:S(2)}, u32[]{:S(2)}) %collective-permute-start.2) | collective-permute-done | bytes 786464 | tf_op jit(solution)/shard_map/ppermute | solution.py:12
  47.2 1.0 pad_maximum_fusion
  48.2 0.0 copy-start
  48.2 1.1 collective-permute-start.3
  49.3 0.7 constant_dynamic-update-slice_fusion.8
  50.0 0.8 constant_dynamic-update-slice_fusion.7
  50.8 1.0 constant_dynamic-update-slice_fusion.6
  51.8 67.3 %collective-permute-done.3 = bf16[128,6144]{1,0:T(8,128)(2,1)S(1)} collective-permute-done((bf16[128,6144]{1,0:T(8,128)(2,1)S(1)}, bf16[128,6144]{1,0:T(8,128)(2,1)S(1)}, u32[]{:S(2)}, u32[]{:S(2)}) %collective-permute-start.3) | collective-permute-done | bytes 1572896 | tf_op jit(solution)/shard_map/ppermute | solution.py:12
  119.0 1.3 constant_dynamic-update-slice_fusion.5
  120.3 0.0 copy-done
  120.3 0.7 constant_dynamic-update-slice_fusion.4
  121.0 0.7 constant_dynamic-update-slice_fusion.3
  121.6 0.8 constant_dynamic-update-slice_fusion.2
  122.4 0.9 constant_dynamic-update-slice_fusion.1
  123.4 1.3 constant_dynamic-update-slice_fusion
  124.6 18.8 %fusion.8 = f32[256,3072]{1,0:T(8,128)} fusion(bf16[6144,3072]{1,0:T(8,128)(2,1)} %param.6, bf16[512,6144]{1,0:T(8,128)(2,1)} %constant_dynamic-update-slice_fusion, s32[]{:T(128)S(6)} %select_n.14), kind=kOutput, calls=%fused_computation.9 | convolution fusion | flops 9663676416 | bytes 44040196 | tf_op jit(solution)/shard_map/dot_general | solution.py:20
  143.5 0.0 copy-start.2
  143.5 0.0 all-reduce.2.cloned.1.call-update
  143.5 0.0 reduce-scatter.2.cloned.1.call-start
  143.5 0.6 copy-done.2
  144.2 83.5 %all-reduce.2.cloned.1.call-done = f32[256,3072]{1,0:T(8,128)} async-done(((f32[256,3072]{1,0:T(8,128)}), f32[256,3072]{1,0:T(8,128)}) %all-reduce.2.cloned.1.call-update) | async-done | bytes 3145744 | tf_op jit(solution)/shard_map/psum | solution.py:24
  227.7 20.0 %fusion.10 = f32[256,6144]{1,0:T(8,128)} fusion(bf16[3072,6144]{1,0:T(8,128)(2,1)} %param.8, f32[256,3072]{1,0:T(8,128)} %all-reduce.2.cloned.1.call-done, f32[3072]{0:T(1024)S(1)} %convert_element_type.12), kind=kOutput, calls=%fused_computation.11 | convolution fusion | flops 9671540736 | bytes 47198208 | tf_op jit(solution)/shard_map/dot_general | solution.py:27
  247.7 0.0 copy-start.1
  247.7 0.0 reduce-scatter.2.cloned.1.call-update
  247.7 0.7 copy-done.1
  248.4 84.7 %reduce-scatter.2.cloned.1.call-done = f32[16,6144]{1,0:T(8,128)} async-done(((f32[256,6144]{1,0:T(8,128)}), f32[16,6144]{1,0:T(8,128)}) %reduce-scatter.2.cloned.1.call-update) | async-done | bytes 393232 | tf_op jit(solution)/shard_map/reduce_scatter | solution.py:26
  333.1 1.7 add_convert_fusion
  (2 shorter events, 0.0 us)
Async XLA Ops:
  6.5 221.1 %all-reduce.2.cloned.1.call-start = ((), (), s32[]{:S(2)}) async-start(), calls=%async_computation.1 | async-start | bytes 6291456 | tf_op jit(solution)/shard_map/psum | solution.py:24
  6.5 8.9 %collective-permute-start = (bf16[16,6144]{1,0:T(8,128)(2,1)}, bf16[16,6144]{1,0:T(8,128)(2,1)S(1)}, u32[]{:S(2)}, u32[]{:S(2)}) collective-permute-start(bf16[16,6144]{1,0:T(8,128)(2,1)} %param.5), channel_id=1, source_target_pairs={{0,30},{2,0},{4,2},{6,4},{8,6},{10,8},{12,10},{14,12},{16,14},{18,... | collective-permute-start | bytes 589832 | tf_op jit(solution)/shard_map/ppermute | solution.py:12
  16.4 9.4 %collective-permute-start.1 = (bf16[32,6144]{1,0:T(8,128)(2,1)S(1)}, bf16[32,6144]{1,0:T(8,128)(2,1)S(1)}, u32[]{:S(2)}, u32[]{:S(2)}) collective-permute-start(bf16[32,6144]{1,0:T(8,128)(2,1)S(1)} %pad_maximum_fusion.2), channel_id=1, source_target_pairs={{0,28},{2,30},{4,0},{6,2},{8,4},{10,6},{12,8},{14,10},{16,12},{18,... | collective-permute-start | bytes 1179656 | tf_op jit(solution)/shard_map/ppermute | solution.py:12
  26.8 20.3 %collective-permute-start.2 = (bf16[64,6144]{1,0:T(8,128)(2,1)S(1)}, bf16[64,6144]{1,0:T(8,128)(2,1)S(1)}, u32[]{:S(2)}, u32[]{:S(2)}) collective-permute-start(bf16[64,6144]{1,0:T(8,128)(2,1)S(1)} %pad_maximum_fusion.1), channel_id=1, source_target_pairs={{0,24},{2,26},{4,28},{6,30},{8,0},{10,2},{12,4},{14,6},{16,8},{18,... | collective-permute-start | bytes 2359304 | tf_op jit(solution)/shard_map/ppermute | solution.py:12
  48.2 72.1 %copy-start = (bf16[16,6144]{1,0:T(8,128)(2,1)S(1)}, bf16[16,6144]{1,0:T(8,128)(2,1)}, u32[]{:S(2)}) copy-start(bf16[16,6144]{1,0:T(8,128)(2,1)} %param.5) | copy-start | bytes 589828
  48.2 70.8 %collective-permute-start.3 = (bf16[128,6144]{1,0:T(8,128)(2,1)S(1)}, bf16[128,6144]{1,0:T(8,128)(2,1)S(1)}, u32[]{:S(2)}, u32[]{:S(2)}) collective-permute-start(bf16[128,6144]{1,0:T(8,128)(2,1)S(1)} %pad_maximum_fusion), channel_id=1, source_target_pairs={{0,16},{2,18},{4,20},{6,22},{8,24},{10,26},{12,28},{14,30},{16,0},... | collective-permute-start | bytes 4718600 | tf_op jit(solution)/shard_map/ppermute | solution.py:12
  143.5 0.7 copy-start.2
  143.5 189.6 %reduce-scatter.2.cloned.1.call-start = ((), (), s32[]{:S(2)}) async-start(), calls=%async_computation.2 | async-start | bytes 6684672 | tf_op jit(solution)/shard_map/reduce_scatter | solution.py:26
  247.7 0.7 copy-start.1
Sparse Core Ops, SparseCore 0:
  143.6 84.0 all-reduce.1
  247.8 85.1 reduce-scatter.1
